TPU v7x, 128 devices: a whole 4x4x4 slice. The times are simulated.
128 devices in a mesh: wide: 16 (over y_lo, z, core), narrow: 8 (over x, y_hi).
Axes of the slice: x: 4, y: 4 (y_hi: 2, y_lo: 2; y = y_hi * 2 + y_lo), z: 4, core: 2. Of those that a mesh axis runs over, the one named last changes fastest.
Arguments:
- fields: float32 [5, 16, 64, 256], P(None, 'wide', 'narrow'), may hold values from -2.1 to 6.1, as said below
- prior_modes: bfloat16 [124, 5, 16, 16384], P(None, None, 'wide', 'narrow'), may hold values from -360 to 360, as said below
Outputs:
- flow_state: float32 [5, 16, 64, 256], P(None, 'wide', 'narrow')
- factor: float32 [128, 128], replicated
Inputs may be any that keep to these rules, and one draw needn't show every extreme that they name: `fields`: density and pressure lie in 0.6 to 1.4, each velocity component below 1.5 in magnitude. `prior_modes`: the columns are linearly independent.
All inputs are finite; a program needn't handle non-finite values.
Results may differ from a plain program's by a relative error of at most 0.0014.
Values may be sent and summed in bfloat16 or wider, within the bound.
No kernel may reach another device: no remote copies, remote signals or barrier semaphores. Data moves between devices by JAX's collectives and lax.ppermute only.
A program may use at most 64 MiB of HBM per device.

v0:
```python
import jax
import jax.numpy as jnp
from jax import lax
from jax.sharding import PartitionSpec as P

STEPS = 2
GAMMA = 1.4
TIME_STEP = 0.25
VISCOSITY = 0.15


def extended(block, sides, width):
    for axis, dim in sides:
        count = lax.axis_size(axis)
        forward = [(i, i + 1) for i in range(count - 1)]
        forward.append((count - 1, 0))
        backward = [(target, source) for source, target in forward]
        low = lax.ppermute(
            lax.slice_in_dim(block, block.shape[dim] - width, None, axis=dim), axis, forward
        )
        high = lax.ppermute(lax.slice_in_dim(block, 0, width, axis=dim), axis, backward)
        block = jnp.concatenate([low, block, high], axis=dim)
    return block


def flux_of(current, dim_index):
    density = current[0]
    momentum = current[1:4]
    energy = current[4]
    vel_d = momentum[dim_index] / density
    pressure = (GAMMA - 1.0) * (
        energy
        - 0.5
        * (momentum[0] * momentum[0] + momentum[1] * momentum[1] + momentum[2] * momentum[2])
        / density
    )
    components = [
        momentum[dim_index],
        momentum[0] * vel_d,
        momentum[1] * vel_d,
        momentum[2] * vel_d,
        (energy + pressure) * vel_d,
    ]
    components[1 + dim_index] = components[1 + dim_index] + pressure
    return jnp.stack(components)


def tendency(current):
    padded = extended(current.astype(jnp.bfloat16), (("wide", 1), ("narrow", 2)), 1).astype(
        current.dtype
    )
    flux_x = flux_of(padded[:, :, 1:-1], 0)
    flux_y = flux_of(padded[:, 1:-1, :], 1)
    flux_z = flux_of(current, 2)
    divergence = (
        flux_x[:, 2:]
        - flux_x[:, :-2]
        + (flux_y[:, :, 2:] - flux_y[:, :, :-2])
        + (jnp.roll(flux_z, -1, 3) - jnp.roll(flux_z, 1, 3))
    )
    laplace = (
        padded[:, 2:, 1:-1]
        + padded[:, :-2, 1:-1]
        + padded[:, 1:-1, 2:]
        + padded[:, 1:-1, :-2]
        + jnp.roll(current, -1, 3)
        + jnp.roll(current, 1, 3)
        - 6.0 * current
    )
    return -0.5 * divergence + VISCOSITY * laplace


def local(fields, prior_modes):
    wide_count = lax.axis_size("wide")
    narrow_count = lax.axis_size("narrow")
    cells_x, cells_y, cells_z = (fields.shape[1], fields.shape[2], fields.shape[3])
    inverse_cells = 1.0 / (cells_x * wide_count * cells_y * narrow_count * cells_z)
    flat_modes = prior_modes.reshape(prior_modes.shape[0], -1)
    contract = (((1,), (1,)), ((), ()))
    gram_modes = lax.dot_general(
        flat_modes, flat_modes, contract, preferred_element_type=jnp.float32
    )
    current = fields
    snapshots = []
    for step_index in range(STEPS):
        section_one = current + TIME_STEP * tendency(current)
        snapshots.append(section_one.astype(jnp.bfloat16))
        current = 0.5 * current + 0.5 * (section_one + TIME_STEP * tendency(section_one))
        snapshots.append(current.astype(jnp.bfloat16))
    arrived = lax.all_to_all(
        jnp.stack(snapshots), "narrow", split_axis=4, concat_axis=3, tiled=True
    )
    snap_rows = jnp.swapaxes(arrived, 3, 4).reshape(arrived.shape[0], -1)
    cross_gram = lax.dot_general(
        flat_modes, snap_rows, contract, preferred_element_type=jnp.float32
    )
    snap_gram = lax.dot_general(snap_rows, snap_rows, contract, preferred_element_type=jnp.float32)
    gram_local = jnp.concatenate(
        [
            jnp.concatenate([gram_modes, cross_gram], 1),
            jnp.concatenate([cross_gram.T, snap_gram], 1),
        ],
        0,
    )
    gram_local = gram_local * inverse_cells
    gram_whole = lax.psum(gram_local, ("wide", "narrow"))
    factor = jnp.linalg.cholesky(gram_whole).T
    return (current, factor)


def solution(mesh):
    placed = (P(None, "wide", "narrow", None), P(None, None, "wide", "narrow"))
    return jax.shard_map(
        local,
        mesh=mesh,
        in_specs=placed,
        out_specs=(P(None, "wide", "narrow", None), P()),
        check_vma=False,
    )
```

profile of v0, /device:TPU:1, one launch (start us, length us, event | category | flops | bytes accessed | tf_op | source)
XLA Modules:
  0.0 256.1 jit_solution(13830206497082720852)
XLA Ops:
  7.2 0.8 convert_element_type.30
  7.9 1.4 collective-permute-start.1
  9.3 1.6 collective-permute-start
  11.7 0.8 constant_dynamic-update-slice_fusion.13
  14.6 0.9 fusion.98
  15.7 5.2 %collective-permute-start.3 = (bf16[5,3,1,256]{3,1,2,0:T(4,128)(2,1)S(1)}, bf16[5,3,1,256]{3,1,2,0:T(4,128)(2,1)S(1)}, u32[]{:S(2)}, u32[]{:S(2)}) collective-permute-start(bf16[5,3,1,256]{3,1,2,0:T(4,128)(2,1)S(1)} %copy.427), channel_id=1, source_target_pairs={{1,0},{2,1},{3,2},{4,3},{5,4},{6,5},{7,6},{0,7},{9,8},{10,9},{11,1... | collective-permute-start | bytes 23048 | tf_op jit(solution)/shard_map/ppermute | solution.py:21
  20.8 0.8 fusion.99
  21.7 5.3 %collective-permute-done.2 = bf16[5,3,1,256]{3,1,2,0:T(4,128)(2,1)S(1)} collective-permute-done((bf16[5,3,1,256]{3,1,2,0:T(4,128)(2,1)S(1)}, bf16[5,3,1,256]{3,1,2,0:T(4,128)(2,1)S(1)}, u32[]{:S(2)}, u32[]{:S(2)}) %collective-permute-start.2) | collective-permute-done | bytes 7712 | tf_op jit(solution)/shard_map/ppermute | solution.py:18
  27.3 0.9 fusion.83
  28.2 4.9 %collective-permute-start.5 = (bf16[5,1,8,256]{3,2,0,1:T(8,128)(2,1)S(1)}, bf16[5,1,8,256]{3,2,0,1:T(8,128)(2,1)S(1)}, u32[]{:S(2)}, u32[]{:S(2)}) collective-permute-start(bf16[5,1,8,256]{3,2,0,1:T(8,128)(2,1)S(1)} %get-tuple-element.65), channel_id=1, source_target_pairs={{8,0},{16,8},{24,16},{32,24},{40,32},{48,40},{56,48},{64,56},{72,6... | collective-permute-start | bytes 61448 | tf_op jit(solution)/shard_map/ppermute | solution.py:21
  33.9 1.0 collective-permute-done.4
  35.6 2.3 collective-permute-start.6
  38.0 1.1 collective-permute-done.7
  39.1 2.6 %collective-permute-done.6 = bf16[5,3,1,256]{3,1,2,0:T(4,128)(2,1)S(1)} collective-permute-done((bf16[5,3,1,256]{3,1,2,0:T(4,128)(2,1)S(1)}, bf16[5,3,1,256]{3,1,2,0:T(4,128)(2,1)S(1)}, u32[]{:S(2)}, u32[]{:S(2)}) %collective-permute-start.6) | collective-permute-done | bytes 7712 | tf_op jit(solution)/shard_map/ppermute | solution.py:18
  42.3 6.1 %collective-permute-start.9 = (bf16[5,1,8,256]{3,2,0,1:T(8,128)(2,1)S(1)}, bf16[5,1,8,256]{3,2,0,1:T(8,128)(2,1)S(1)}, u32[]{:S(2)}, u32[]{:S(2)}) collective-permute-start(bf16[5,1,8,256]{3,2,0,1:T(8,128)(2,1)S(1)} %fusion.78), channel_id=1, source_target_pairs={{8,0},{16,8},{24,16},{32,24},{40,32},{48,40},{56,48},{64,56},{72,6... | collective-permute-start | bytes 61448 | tf_op jit(solution)/shard_map/ppermute | solution.py:21
  49.8 2.9 %collective-permute-start.10 = (bf16[5,3,1,256]{3,1,2,0:T(4,128)(2,1)S(1)}, bf16[5,3,1,256]{3,1,2,0:T(4,128)(2,1)S(1)}, u32[]{:S(2)}, u32[]{:S(2)}) collective-permute-start(bf16[5,3,1,256]{3,1,2,0:T(4,128)(2,1)S(1)} %copy.394), channel_id=1, source_target_pairs={{0,1},{1,2},{2,3},{3,4},{4,5},{5,6},{6,7},{7,0},{8,9},{9,10},{10,1... | collective-permute-start | bytes 23048 | tf_op jit(solution)/shard_map/ppermute | solution.py:18
  52.8 1.0 collective-permute-done.11
  53.8 2.2 collective-permute-done.10
  56.4 5.4 %collective-permute-start.13 = (bf16[5,1,8,256]{3,2,0,1:T(8,128)(2,1)S(1)}, bf16[5,1,8,256]{3,2,0,1:T(8,128)(2,1)S(1)}, u32[]{:S(2)}, u32[]{:S(2)}) collective-permute-start(bf16[5,1,8,256]{3,2,0,1:T(8,128)(2,1)S(1)} %get-tuple-element.31), channel_id=1, source_target_pairs={{8,0},{16,8},{24,16},{32,24},{40,32},{48,40},{56,48},{64,56},{72,6... | collective-permute-start | bytes 61448 | tf_op jit(solution)/shard_map/ppermute | solution.py:21
  63.2 2.9 %collective-permute-start.14 = (bf16[5,3,1,256]{3,1,2,0:T(4,128)(2,1)S(1)}, bf16[5,3,1,256]{3,1,2,0:T(4,128)(2,1)S(1)}, u32[]{:S(2)}, u32[]{:S(2)}) collective-permute-start(bf16[5,3,1,256]{3,1,2,0:T(4,128)(2,1)S(1)} %copy.405), channel_id=1, source_target_pairs={{0,1},{1,2},{2,3},{3,4},{4,5},{5,6},{6,7},{7,0},{8,9},{9,10},{10,1... | collective-permute-start | bytes 23048 | tf_op jit(solution)/shard_map/ppermute | solution.py:18
  66.2 1.0 collective-permute-done.15
  67.2 2.2 collective-permute-done.14
  71.2 2.1 reshape.630
  73.3 3.4 %all-to-all-start = ((bf16[8,2,2560]{2,1,0:T(2,128)(2,1)}), bf16[8,2,2560]{2,1,0:T(2,128)(2,1)S(1)}, u32[]{:S(2)}, u32[]{:S(2)}) async-start(bf16[8,2,2560]{2,1,0:T(2,128)(2,1)} %reshape.630), calls=%async_computation | async-start | bytes 163840 | tf_op jit(solution)/shard_map/all_to_all | solution.py:90
  76.9 3.4 %fusion.2 = f32[124,124]{0,1:T(8,128)S(1)} fusion(bf16[124,5,1,2048]{3,0,2,1:T(8,128)(2,1)} %param.3), kind=kOutput, calls=%fused_computation.2 | convolution fusion | flops 314900480 | bytes 2601024 | tf_op jit(solution)/shard_map/dot_general | solution.py:80
  80.2 3.3 %copy.420 = bf16[124,5,1,2048]{0,3,1,2:T(8,128)(2,1)S(1)} copy(bf16[124,5,1,2048]{3,0,2,1:T(8,128)(2,1)} %param.3) | data formatting | bytes 5079040 | tf_op args[1]
  83.6 2.6 %reshape.631 = bf16[256,5,1,4,8]{4,3,2,1,0:T(4,128)(2,1)} reshape(bf16[8,2,2560]{2,1,0:T(2,128)(2,1)S(1)} %all-to-all-done) | data formatting | bytes 163840
  86.2 1.8 copy.417
  90.1 143.6 %all-reduce.2.cloned.1.call-done = f32[128,128]{0,1:T(8,128)} async-done(((f32[128,128]{0,1:T(8,128)}), f32[128,128]{0,1:T(8,128)}) %all-reduce.2.cloned.1.call-update) | async-done | bytes 65552 | tf_op jit(solution)/shard_map/psum | solution.py:106
  233.7 0.9 copy.422
  234.6 0.9 fusion.6
  235.5 11.7 %cholesky.18 = f32[128,128]{1,0:T(8,128)S(1)} custom-call(f32[128,128]{1,0:T(8,128)S(1)} %fusion.6), custom_call_target="Cholesky" | custom-call | tf_op jit(solution)/shard_map/jit(cholesky)/cholesky | solution.py:107
  (135 shorter events, 14.4 us)
Async XLA Ops:
  7.9 7.6 %collective-permute-start.1 = (bf16[5,1,8,256]{3,2,1,0:T(8,128)(2,1)S(1)}, bf16[5,1,8,256]{3,2,1,0:T(8,128)(2,1)S(1)}, u32[]{:S(2)}, u32[]{:S(2)}) collective-permute-start(bf16[5,1,8,256]{3,2,1,0:T(8,128)(2,1)S(1)} %convert_element_type.30), channel_id=1, source_target_pairs={{8,0},{16,8},{24,16},{32,24},{40,32},{48,40},{56,48},{64,56},{72,6... | collective-permute-start | bytes 61448 | tf_op jit(solution)/shard_map/ppermute | solution.py:21
  9.3 6.3 %collective-permute-start = (bf16[5,1,8,256]{3,2,1,0:T(8,128)(2,1)S(1)}, bf16[5,1,8,256]{3,2,1,0:T(8,128)(2,1)S(1)}, u32[]{:S(2)}, u32[]{:S(2)}) collective-permute-start(bf16[5,1,8,256]{3,2,1,0:T(8,128)(2,1)S(1)} %convert_element_type.30), channel_id=1, source_target_pairs={{0,8},{8,16},{16,24},{24,32},{32,40},{40,48},{48,56},{56,64},{64,7... | collective-permute-start | bytes 61448 | tf_op jit(solution)/shard_map/ppermute | solution.py:18
  11.7 30.4 %copy-start = (f32[5,1,8,256]{3,2,1,0:T(8,128)S(1)}, f32[5,1,8,256]{3,2,1,0:T(8,128)}, u32[]{:S(2)}) copy-start(f32[5,1,8,256]{3,2,1,0:T(8,128)} %param.2) | copy-start | bytes 122884
  15.7 6.0 %collective-permute-start.3 = (bf16[5,3,1,256]{3,1,2,0:T(4,128)(2,1)S(1)}, bf16[5,3,1,256]{3,1,2,0:T(4,128)(2,1)S(1)}, u32[]{:S(2)}, u32[]{:S(2)}) collective-permute-start(bf16[5,3,1,256]{3,1,2,0:T(4,128)(2,1)S(1)} %copy.427), channel_id=1, source_target_pairs={{1,0},{2,1},{3,2},{4,3},{5,4},{6,5},{7,6},{0,7},{9,8},{10,9},{11,1... | collective-permute-start | bytes 23048 | tf_op jit(solution)/shard_map/ppermute | solution.py:21
  20.8 6.1 %collective-permute-start.2 = (bf16[5,3,1,256]{3,1,2,0:T(4,128)(2,1)S(1)}, bf16[5,3,1,256]{3,1,2,0:T(4,128)(2,1)S(1)}, u32[]{:S(2)}, u32[]{:S(2)}) collective-permute-start(bf16[5,3,1,256]{3,1,2,0:T(4,128)(2,1)S(1)} %copy.426), channel_id=1, source_target_pairs={{0,1},{1,2},{2,3},{3,4},{4,5},{5,6},{6,7},{7,0},{8,9},{9,10},{10,1... | collective-permute-start | bytes 23048 | tf_op jit(solution)/shard_map/ppermute | solution.py:18
  28.2 5.7 %collective-permute-start.5 = (bf16[5,1,8,256]{3,2,0,1:T(8,128)(2,1)S(1)}, bf16[5,1,8,256]{3,2,0,1:T(8,128)(2,1)S(1)}, u32[]{:S(2)}, u32[]{:S(2)}) collective-permute-start(bf16[5,1,8,256]{3,2,0,1:T(8,128)(2,1)S(1)} %get-tuple-element.65), channel_id=1, source_target_pairs={{8,0},{16,8},{24,16},{32,24},{40,32},{48,40},{56,48},{64,56},{72,6... | collective-permute-start | bytes 61448 | tf_op jit(solution)/shard_map/ppermute | solution.py:21
  33.0 1.8 collective-permute-start.4
  34.9 4.2 %collective-permute-start.7 = (bf16[5,3,1,256]{3,1,2,0:T(4,128)(2,1)S(1)}, bf16[5,3,1,256]{3,1,2,0:T(4,128)(2,1)S(1)}, u32[]{:S(2)}, u32[]{:S(2)}) collective-permute-start(bf16[5,3,1,256]{3,1,2,0:T(4,128)(2,1)S(1)} %copy.383), channel_id=1, source_target_pairs={{1,0},{2,1},{3,2},{4,3},{5,4},{6,5},{7,6},{0,7},{9,8},{10,9},{11,1... | collective-permute-start | bytes 23048 | tf_op jit(solution)/shard_map/ppermute | solution.py:21
  35.6 6.1 %collective-permute-start.6 = (bf16[5,3,1,256]{3,1,2,0:T(4,128)(2,1)S(1)}, bf16[5,3,1,256]{3,1,2,0:T(4,128)(2,1)S(1)}, u32[]{:S(2)}, u32[]{:S(2)}) collective-permute-start(bf16[5,3,1,256]{3,1,2,0:T(4,128)(2,1)S(1)} %copy.382), channel_id=1, source_target_pairs={{0,1},{1,2},{2,3},{3,4},{4,5},{5,6},{6,7},{7,0},{8,9},{9,10},{10,1... | collective-permute-start | bytes 23048 | tf_op jit(solution)/shard_map/ppermute | solution.py:18
  42.3 7.0 %collective-permute-start.9 = (bf16[5,1,8,256]{3,2,0,1:T(8,128)(2,1)S(1)}, bf16[5,1,8,256]{3,2,0,1:T(8,128)(2,1)S(1)}, u32[]{:S(2)}, u32[]{:S(2)}) collective-permute-start(bf16[5,1,8,256]{3,2,0,1:T(8,128)(2,1)S(1)} %fusion.78), channel_id=1, source_target_pairs={{8,0},{16,8},{24,16},{32,24},{40,32},{48,40},{56,48},{64,56},{72,6... | collective-permute-start | bytes 61448 | tf_op jit(solution)/shard_map/ppermute | solution.py:21
  48.5 1.2 collective-permute-start.8
  49.7 4.1 %collective-permute-start.11 = (bf16[5,3,1,256]{3,1,2,0:T(4,128)(2,1)S(1)}, bf16[5,3,1,256]{3,1,2,0:T(4,128)(2,1)S(1)}, u32[]{:S(2)}, u32[]{:S(2)}) collective-permute-start(bf16[5,3,1,256]{3,1,2,0:T(4,128)(2,1)S(1)} %copy.395), channel_id=1, source_target_pairs={{1,0},{2,1},{3,2},{4,3},{5,4},{6,5},{7,6},{0,7},{9,8},{10,9},{11,1... | collective-permute-start | bytes 23048 | tf_op jit(solution)/shard_map/ppermute | solution.py:21
  49.8 6.2 %collective-permute-start.10 = (bf16[5,3,1,256]{3,1,2,0:T(4,128)(2,1)S(1)}, bf16[5,3,1,256]{3,1,2,0:T(4,128)(2,1)S(1)}, u32[]{:S(2)}, u32[]{:S(2)}) collective-permute-start(bf16[5,3,1,256]{3,1,2,0:T(4,128)(2,1)S(1)} %copy.394), channel_id=1, source_target_pairs={{0,1},{1,2},{2,3},{3,4},{4,5},{5,6},{6,7},{7,0},{8,9},{9,10},{10,1... | collective-permute-start | bytes 23048 | tf_op jit(solution)/shard_map/ppermute | solution.py:18
  56.4 6.3 %collective-permute-start.13 = (bf16[5,1,8,256]{3,2,0,1:T(8,128)(2,1)S(1)}, bf16[5,1,8,256]{3,2,0,1:T(8,128)(2,1)S(1)}, u32[]{:S(2)}, u32[]{:S(2)}) collective-permute-start(bf16[5,1,8,256]{3,2,0,1:T(8,128)(2,1)S(1)} %get-tuple-element.31), channel_id=1, source_target_pairs={{8,0},{16,8},{24,16},{32,24},{40,32},{48,40},{56,48},{64,56},{72,6... | collective-permute-start | bytes 61448 | tf_op jit(solution)/shard_map/ppermute | solution.py:21
  61.9 1.2 collective-permute-start.12
  63.1 4.1 %collective-permute-start.15 = (bf16[5,3,1,256]{3,1,2,0:T(4,128)(2,1)S(1)}, bf16[5,3,1,256]{3,1,2,0:T(4,128)(2,1)S(1)}, u32[]{:S(2)}, u32[]{:S(2)}) collective-permute-start(bf16[5,3,1,256]{3,1,2,0:T(4,128)(2,1)S(1)} %copy.406), channel_id=1, source_target_pairs={{1,0},{2,1},{3,2},{4,3},{5,4},{6,5},{7,6},{0,7},{9,8},{10,9},{11,1... | collective-permute-start | bytes 23048 | tf_op jit(solution)/shard_map/ppermute | solution.py:21
  63.2 6.2 %collective-permute-start.14 = (bf16[5,3,1,256]{3,1,2,0:T(4,128)(2,1)S(1)}, bf16[5,3,1,256]{3,1,2,0:T(4,128)(2,1)S(1)}, u32[]{:S(2)}, u32[]{:S(2)}) collective-permute-start(bf16[5,3,1,256]{3,1,2,0:T(4,128)(2,1)S(1)} %copy.405), channel_id=1, source_target_pairs={{0,1},{1,2},{2,3},{3,4},{4,5},{5,6},{6,7},{7,0},{8,9},{9,10},{10,1... | collective-permute-start | bytes 23048 | tf_op jit(solution)/shard_map/ppermute | solution.py:18
  73.3 10.3 %all-to-all-start = ((bf16[8,2,2560]{2,1,0:T(2,128)(2,1)}), bf16[8,2,2560]{2,1,0:T(2,128)(2,1)S(1)}, u32[]{:S(2)}, u32[]{:S(2)}) async-start(bf16[8,2,2560]{2,1,0:T(2,128)(2,1)} %reshape.630), calls=%async_computation | async-start | bytes 163840 | tf_op jit(solution)/shard_map/all_to_all | solution.py:90
  76.6 157.1 %all-reduce.2.cloned.1.call-start = ((), (), s32[]{:S(2)}) async-start(), calls=%async_computation.1 | async-start | bytes 131072 | tf_op jit(solution)/shard_map/psum | solution.py:106
Sparse Core Ops, SparseCore 0:
  90.2 143.4 all-reduce.1
where the time goes:
time: 257 us; the launch traced here: 256 us
  waiting for transfers between devices  162 us (63%)
  starting transfers between devices  37.3 us (15%)
  other arithmetic  21.4 us (8%)
  local copies, waits for them, and re-layouts  16.3 us (6%)
  between operations  14.7 us (6%)
  matrix products  4.08 us (2%)
    psum x1, waiting for transfers between devices, local(): gram_whole = lax.psum(gram_local, ('wide', 'narrow'))  144 us
    ppermute x8, starting transfers between devices, extended(): lax.ppermute(lax.slice_in_dim(block, 0, width, axis=dim), axis, backward)  23.8 us
    ppermute x8, waiting for transfers between devices, extended(): lax.ppermute(lax.slice_in_dim(block, block.shape[dim] - width, None, axis...  13.9 us
    another operation x3, other arithmetic, local(): factor = jnp.linalg.cholesky(gram_whole).T  12.4 us
    ppermute x8, starting transfers between devices, extended(): lax.ppermute(lax.slice_in_dim(block, block.shape[dim] - width, None, axis...  9.89 us
    unnamed x16, local copies, waits for them, and re-layouts  9.47 us
  transfers between devices with their start and end apart: 18, of which 14 were waited for; matrix products, arithmetic and copies ran while one was open for 5% of the time, Pallas kernels for 0%

commit v1 on v0

--- a/solution.py
+++ b/solution.py
@@ -71,6 +71,10 @@
 
 
 def local(fields, prior_modes):
+
+    def _use_columns(sheet):
+        return jnp.sum(jax.lax.all_gather(sheet, axis_name=("wide", "narrow")), axis=0)
+
     wide_count = lax.axis_size("wide")
     narrow_count = lax.axis_size("narrow")
     cells_x, cells_y, cells_z = (fields.shape[1], fields.shape[2], fields.shape[3])
@@ -103,7 +107,7 @@
         0,
     )
     gram_local = gram_local * inverse_cells
-    gram_whole = lax.psum(gram_local, ("wide", "narrow"))
+    gram_whole = _use_columns(gram_local)
     factor = jnp.linalg.cholesky(gram_whole).T
     return (current, factor)
 

time: 257 us -> 429 us (1.67)
  waiting for transfers between devices: 162 us -> 332 us
    all_gather x0 -> x1, waiting for transfers between devices: none -> 314 us  [_use_columns(): jax.lax.all_gather(sheet, axis_name=('wide', 'narrow'))]
    psum x1 -> x0, waiting for transfers between devices: 144 us -> none  [local(): gram_whole = lax.psum(gram_local, ('wide', 'narrow'))]
  transfers between devices with their start and end apart: 18 -> 18, of which waited for: 14 -> 14; matrix products, arithmetic and copies ran while one was open for 5% -> 3% of each run, Pallas kernels for 0% -> 0%
where the time goes in v1:
time: 429 us; the launch traced here: 428 us
  waiting for transfers between devices  332 us (77%)
  starting transfers between devices  37.3 us (9%)
  other arithmetic  23.7 us (6%)
  local copies, waits for them, and re-layouts  16.1 us (4%)
  between operations  14.7 us (3%)
    all_gather x1, waiting for transfers between devices, _use_columns(): jax.lax.all_gather(sheet, axis_name=('wide', 'narrow'))  314 us
    ppermute x8, starting transfers between devices, extended(): lax.ppermute(lax.slice_in_dim(block, 0, width, axis=dim), axis, backward)  23.8 us
    ppermute x8, waiting for transfers between devices, extended(): lax.ppermute(lax.slice_in_dim(block, block.shape[dim] - width, None, axis...  13.9 us
    another operation x3, other arithmetic, local(): factor = jnp.linalg.cholesky(gram_whole).T  12.4 us
    ppermute x8, starting transfers between devices, extended(): lax.ppermute(lax.slice_in_dim(block, block.shape[dim] - width, None, axis...  9.89 us
    unnamed x16, local copies, waits for them, and re-layouts  9.4 us
  transfers between devices with their start and end apart: 18, of which 14 were waited for; matrix products, arithmetic and copies ran while one was open for 3% of the time, Pallas kernels for 0%

profile of v1, /device:TPU:1, one launch (start us, length us, event | category | flops | bytes accessed | tf_op | source)
XLA Modules:
  0.0 428.2 jit_solution(15845789211913904846)
XLA Ops:
  7.2 0.8 convert_element_type.30
  7.9 1.4 collective-permute-start.1
  9.3 1.6 collective-permute-start
  11.7 0.8 constant_dynamic-update-slice_fusion.13
  13.1 0.8 constant_dynamic-update-slice_fusion.11
  14.6 0.9 fusion.98
  15.7 5.2 %collective-permute-start.3 = (bf16[5,3,1,256]{3,1,2,0:T(4,128)(2,1)S(1)}, bf16[5,3,1,256]{3,1,2,0:T(4,128)(2,1)S(1)}, u32[]{:S(2)}, u32[]{:S(2)}) collective-permute-start(bf16[5,3,1,256]{3,1,2,0:T(4,128)(2,1)S(1)} %copy.431), channel_id=1, source_target_pairs={{1,0},{2,1},{3,2},{4,3},{5,4},{6,5},{7,6},{0,7},{9,8},{10,9},{11,1... | collective-permute-start | bytes 23048 | tf_op jit(solution)/shard_map/ppermute | solution.py:21
  20.9 0.8 fusion.99
  21.7 5.3 %collective-permute-done.2 = bf16[5,3,1,256]{3,1,2,0:T(4,128)(2,1)S(1)} collective-permute-done((bf16[5,3,1,256]{3,1,2,0:T(4,128)(2,1)S(1)}, bf16[5,3,1,256]{3,1,2,0:T(4,128)(2,1)S(1)}, u32[]{:S(2)}, u32[]{:S(2)}) %collective-permute-start.2) | collective-permute-done | bytes 7712 | tf_op jit(solution)/shard_map/ppermute | solution.py:18
  27.3 0.9 fusion.83
  28.2 4.9 %collective-permute-start.5 = (bf16[5,1,8,256]{3,2,0,1:T(8,128)(2,1)S(1)}, bf16[5,1,8,256]{3,2,0,1:T(8,128)(2,1)S(1)}, u32[]{:S(2)}, u32[]{:S(2)}) collective-permute-start(bf16[5,1,8,256]{3,2,0,1:T(8,128)(2,1)S(1)} %get-tuple-element.65), channel_id=1, source_target_pairs={{8,0},{16,8},{24,16},{32,24},{40,32},{48,40},{56,48},{64,56},{72,6... | collective-permute-start | bytes 61448 | tf_op jit(solution)/shard_map/ppermute | solution.py:21
  33.9 1.0 collective-permute-done.4
  35.6 2.3 collective-permute-start.6
  38.0 1.1 collective-permute-done.7
  39.1 2.6 collective-permute-done.6
  42.2 6.1 %collective-permute-start.9 = (bf16[5,1,8,256]{3,2,0,1:T(8,128)(2,1)S(1)}, bf16[5,1,8,256]{3,2,0,1:T(8,128)(2,1)S(1)}, u32[]{:S(2)}, u32[]{:S(2)}) collective-permute-start(bf16[5,1,8,256]{3,2,0,1:T(8,128)(2,1)S(1)} %fusion.78), channel_id=1, source_target_pairs={{8,0},{16,8},{24,16},{32,24},{40,32},{48,40},{56,48},{64,56},{72,6... | collective-permute-start | bytes 61448 | tf_op jit(solution)/shard_map/ppermute | solution.py:21
  49.7 3.0 collective-permute-start.10
  52.7 1.0 collective-permute-done.11
  53.7 2.2 collective-permute-done.10
  56.3 5.4 %collective-permute-start.13 = (bf16[5,1,8,256]{3,2,0,1:T(8,128)(2,1)S(1)}, bf16[5,1,8,256]{3,2,0,1:T(8,128)(2,1)S(1)}, u32[]{:S(2)}, u32[]{:S(2)}) collective-permute-start(bf16[5,1,8,256]{3,2,0,1:T(8,128)(2,1)S(1)} %get-tuple-element.31), channel_id=1, source_target_pairs={{8,0},{16,8},{24,16},{32,24},{40,32},{48,40},{56,48},{64,56},{72,6... | collective-permute-start | bytes 61448 | tf_op jit(solution)/shard_map/ppermute | solution.py:21
  63.1 3.0 collective-permute-start.14
  66.1 1.0 collective-permute-done.15
  67.1 2.2 collective-permute-done.14
  71.1 2.0 reshape.659
  73.1 3.4 all-to-all-start
  76.7 3.4 fusion.2
  80.1 3.3 copy.423
  83.4 2.6 reshape.660
  86.0 1.8 copy.420
  90.0 313.6 %all-gather.2.cloned.1.call-done = f32[128,128,128]{2,1,0:T(8,128)} async-done(((f32[1,128,128]{2,1,0:T(8,128)}), f32[128,128,128]{2,1,0:T(8,128)}) %all-gather.2.cloned.1.call-update) | async-done | bytes 8388624 | tf_op jit(solution)/shard_map/all_gather | solution.py:76
  403.6 3.8 reduce_sum.9
  407.6 11.7 %cholesky.18 = f32[128,128]{1,0:T(8,128)S(1)} custom-call(f32[128,128]{1,0:T(8,128)S(1)} %fusion.6), custom_call_target="Cholesky" | custom-call | tf_op jit(solution)/shard_map/jit(cholesky)/cholesky | solution.py:111
  (138 shorter events, 13.8 us)
Async XLA Ops:
  7.9 7.6 %collective-permute-start.1 = (bf16[5,1,8,256]{3,2,1,0:T(8,128)(2,1)S(1)}, bf16[5,1,8,256]{3,2,1,0:T(8,128)(2,1)S(1)}, u32[]{:S(2)}, u32[]{:S(2)}) collective-permute-start(bf16[5,1,8,256]{3,2,1,0:T(8,128)(2,1)S(1)} %convert_element_type.30), channel_id=1, source_target_pairs={{8,0},{16,8},{24,16},{32,24},{40,32},{48,40},{56,48},{64,56},{72,6... | collective-permute-start | bytes 61448 | tf_op jit(solution)/shard_map/ppermute | solution.py:21
  9.3 6.3 %collective-permute-start = (bf16[5,1,8,256]{3,2,1,0:T(8,128)(2,1)S(1)}, bf16[5,1,8,256]{3,2,1,0:T(8,128)(2,1)S(1)}, u32[]{:S(2)}, u32[]{:S(2)}) collective-permute-start(bf16[5,1,8,256]{3,2,1,0:T(8,128)(2,1)S(1)} %convert_element_type.30), channel_id=1, source_target_pairs={{0,8},{8,16},{16,24},{24,32},{32,40},{40,48},{48,56},{56,64},{64,7... | collective-permute-start | bytes 61448 | tf_op jit(solution)/shard_map/ppermute | solution.py:18
  11.7 30.4 %copy-start = (f32[5,1,8,256]{3,2,1,0:T(8,128)S(1)}, f32[5,1,8,256]{3,2,1,0:T(8,128)}, u32[]{:S(2)}) copy-start(f32[5,1,8,256]{3,2,1,0:T(8,128)} %param.2) | copy-start | bytes 122884
  15.7 6.0 %collective-permute-start.3 = (bf16[5,3,1,256]{3,1,2,0:T(4,128)(2,1)S(1)}, bf16[5,3,1,256]{3,1,2,0:T(4,128)(2,1)S(1)}, u32[]{:S(2)}, u32[]{:S(2)}) collective-permute-start(bf16[5,3,1,256]{3,1,2,0:T(4,128)(2,1)S(1)} %copy.431), channel_id=1, source_target_pairs={{1,0},{2,1},{3,2},{4,3},{5,4},{6,5},{7,6},{0,7},{9,8},{10,9},{11,1... | collective-permute-start | bytes 23048 | tf_op jit(solution)/shard_map/ppermute | solution.py:21
  20.8 6.1 %collective-permute-start.2 = (bf16[5,3,1,256]{3,1,2,0:T(4,128)(2,1)S(1)}, bf16[5,3,1,256]{3,1,2,0:T(4,128)(2,1)S(1)}, u32[]{:S(2)}, u32[]{:S(2)}) collective-permute-start(bf16[5,3,1,256]{3,1,2,0:T(4,128)(2,1)S(1)} %copy.430), channel_id=1, source_target_pairs={{0,1},{1,2},{2,3},{3,4},{4,5},{5,6},{6,7},{7,0},{8,9},{9,10},{10,1... | collective-permute-start | bytes 23048 | tf_op jit(solution)/shard_map/ppermute | solution.py:18
  28.2 5.7 %collective-permute-start.5 = (bf16[5,1,8,256]{3,2,0,1:T(8,128)(2,1)S(1)}, bf16[5,1,8,256]{3,2,0,1:T(8,128)(2,1)S(1)}, u32[]{:S(2)}, u32[]{:S(2)}) collective-permute-start(bf16[5,1,8,256]{3,2,0,1:T(8,128)(2,1)S(1)} %get-tuple-element.65), channel_id=1, source_target_pairs={{8,0},{16,8},{24,16},{32,24},{40,32},{48,40},{56,48},{64,56},{72,6... | collective-permute-start | bytes 61448 | tf_op jit(solution)/shard_map/ppermute | solution.py:21
  33.1 1.8 collective-permute-start.4
  34.9 4.2 collective-permute-start.7
  35.6 6.1 %collective-permute-start.6 = (bf16[5,3,1,256]{3,1,2,0:T(4,128)(2,1)S(1)}, bf16[5,3,1,256]{3,1,2,0:T(4,128)(2,1)S(1)}, u32[]{:S(2)}, u32[]{:S(2)}) collective-permute-start(bf16[5,3,1,256]{3,1,2,0:T(4,128)(2,1)S(1)} %copy.385), channel_id=1, source_target_pairs={{0,1},{1,2},{2,3},{3,4},{4,5},{5,6},{6,7},{7,0},{8,9},{9,10},{10,1... | collective-permute-start | bytes 23048 | tf_op jit(solution)/shard_map/ppermute | solution.py:18
  42.2 7.0 %collective-permute-start.9 = (bf16[5,1,8,256]{3,2,0,1:T(8,128)(2,1)S(1)}, bf16[5,1,8,256]{3,2,0,1:T(8,128)(2,1)S(1)}, u32[]{:S(2)}, u32[]{:S(2)}) collective-permute-start(bf16[5,1,8,256]{3,2,0,1:T(8,128)(2,1)S(1)} %fusion.78), channel_id=1, source_target_pairs={{8,0},{16,8},{24,16},{32,24},{40,32},{48,40},{56,48},{64,56},{72,6... | collective-permute-start | bytes 61448 | tf_op jit(solution)/shard_map/ppermute | solution.py:21
  48.4 1.2 collective-permute-start.8
  49.6 4.1 collective-permute-start.11
  49.7 6.2 %collective-permute-start.10 = (bf16[5,3,1,256]{3,1,2,0:T(4,128)(2,1)S(1)}, bf16[5,3,1,256]{3,1,2,0:T(4,128)(2,1)S(1)}, u32[]{:S(2)}, u32[]{:S(2)}) collective-permute-start(bf16[5,3,1,256]{3,1,2,0:T(4,128)(2,1)S(1)} %copy.397), channel_id=1, source_target_pairs={{0,1},{1,2},{2,3},{3,4},{4,5},{5,6},{6,7},{7,0},{8,9},{9,10},{10,1... | collective-permute-start | bytes 23048 | tf_op jit(solution)/shard_map/ppermute | solution.py:18
  56.3 6.3 %collective-permute-start.13 = (bf16[5,1,8,256]{3,2,0,1:T(8,128)(2,1)S(1)}, bf16[5,1,8,256]{3,2,0,1:T(8,128)(2,1)S(1)}, u32[]{:S(2)}, u32[]{:S(2)}) collective-permute-start(bf16[5,1,8,256]{3,2,0,1:T(8,128)(2,1)S(1)} %get-tuple-element.31), channel_id=1, source_target_pairs={{8,0},{16,8},{24,16},{32,24},{40,32},{48,40},{56,48},{64,56},{72,6... | collective-permute-start | bytes 61448 | tf_op jit(solution)/shard_map/ppermute | solution.py:21
  61.8 1.2 collective-permute-start.12
  63.0 4.1 collective-permute-start.15
  63.1 6.2 %collective-permute-start.14 = (bf16[5,3,1,256]{3,1,2,0:T(4,128)(2,1)S(1)}, bf16[5,3,1,256]{3,1,2,0:T(4,128)(2,1)S(1)}, u32[]{:S(2)}, u32[]{:S(2)}) collective-permute-start(bf16[5,3,1,256]{3,1,2,0:T(4,128)(2,1)S(1)} %copy.408), channel_id=1, source_target_pairs={{0,1},{1,2},{2,3},{3,4},{4,5},{5,6},{6,7},{7,0},{8,9},{9,10},{10,1... | collective-permute-start | bytes 23048 | tf_op jit(solution)/shard_map/ppermute | solution.py:18
  73.1 10.3 %all-to-all-start = ((bf16[8,2,2560]{2,1,0:T(2,128)(2,1)}), bf16[8,2,2560]{2,1,0:T(2,128)(2,1)S(1)}, u32[]{:S(2)}, u32[]{:S(2)}) async-start(bf16[8,2,2560]{2,1,0:T(2,128)(2,1)} %reshape.659), calls=%async_computation | async-start | bytes 163840 | tf_op jit(solution)/shard_map/all_to_all | solution.py:94
  76.5 327.2 %all-gather.2.cloned.1.call-start = ((), (), s32[]{:S(2)}) async-start(), calls=%async_computation.1 | async-start | bytes 8454144 | tf_op jit(solution)/shard_map/all_gather | solution.py:76
Sparse Core Ops, SparseCore 0:
  90.1 313.4 all-gather.1
